TPU v7x, 32 devices: a whole 2x2x4 slice. The times are simulated.
32 devices in a mesh: facet: 4 (over y, x), band: 4 (over z), sub: 2 (over core).
Axes of the slice: x: 2, y: 2, z: 4, core: 2. Of those that a mesh axis runs over, the one named last changes fastest.
Arguments:
- facets: bfloat16 [8192, 2048], P(('facet', 'band')), may hold values from -6 to 6
- window: float32 [2048], replicated, may hold values from 0.5 to 1.5
- facet_offsets: int32 [4, 2], replicated, may hold values from 0 to 49151
- row_offsets: int32 [8], replicated, may hold values from 0 to 49151
- column_offset: int32 [1], replicated, may hold values from 0 to 49151
- kernel: bfloat16 [256, 256], replicated, may hold values from -0.375 to 0.375
- tile_counts: int32 [8, 16, 16], replicated, may hold values from 0 to 32
Outputs:
- residual: bfloat16 [8192, 2048], P(('facet', 'band'))
All inputs are finite; a program needn't handle non-finite values.
Results may differ from a plain program's by a relative error of at most 0.013.
Values may be sent and summed in bfloat16 or wider, within the bound.
A program may use at most 64 MiB of HBM per device.

v0:
```python
import math
import jax
import jax.numpy as jnp
from jax import lax
from jax.sharding import PartitionSpec as P

IMAGE = 49152


def modular_product(first, second):
    upper_bits = first // 256
    lower_bits = first % 256
    reduced = upper_bits * second % IMAGE
    reduced = reduced * 256 % IMAGE
    return (reduced + lower_bits * second) % IMAGE


def phase_table(frequency, position):
    reduced = modular_product(frequency % IMAGE, position % IMAGE)
    angle = reduced.astype(jnp.float32) * (2.0 * math.pi / IMAGE)
    return (jnp.cos(angle), jnp.sin(angle))


def product(left, right):
    return jnp.dot(left, right, preferred_element_type=jnp.float32)


def body(facets, window, facet_offsets, row_offsets, column_offset, kernel, tile_counts):
    facet_count = lax.axis_size("facet")
    band_count = lax.axis_size("band")
    sub_count = lax.axis_size("sub")
    facet_at = lax.axis_index("facet")
    band_at = lax.axis_index("band")
    sub_at = lax.axis_index("sub")
    band_rows = facets.shape[0]
    width = facets.shape[1]
    contrib = kernel.shape[0]
    sub_rows = contrib // band_count
    stacked = band_count * contrib
    a_scale = 1.0 / math.sqrt(width * facet_count)
    b_scale = 1.0 / math.sqrt(width)
    back_scale = 1.0 / math.sqrt(band_count * sub_count * contrib)
    out_scale = 1.0 / math.sqrt(contrib)
    offset = lax.dynamic_slice_in_dim(facet_offsets, facet_at, 1, 0)[0]
    cells = jnp.arange(width, dtype=jnp.int32)
    frequencies = jnp.arange(contrib, dtype=jnp.int32)
    cosine, sine = phase_table(column_offset[0] + frequencies[:, None], offset[1] + cells[None, :])
    col_real = (cosine * window[None, :] * b_scale).astype(jnp.bfloat16)
    col_imag = (-sine * window[None, :] * b_scale).astype(jnp.bfloat16)
    t_real = jnp.einsum("xy,ky->xk", facets, col_real, preferred_element_type=jnp.float32).astype(
        jnp.bfloat16
    )
    t_imag = jnp.einsum("xy,ky->xk", facets, col_imag, preferred_element_type=jnp.float32).astype(
        jnp.bfloat16
    )
    starts = lax.dynamic_slice_in_dim(row_offsets, sub_at * band_count, band_count, 0)
    row_freqs = (starts[:, None] + frequencies[None, :]).reshape(stacked)
    positions = offset[0] + band_at * band_rows + jnp.arange(band_rows, dtype=jnp.int32)
    row_cos, row_sin = phase_table(row_freqs[:, None], positions[None, :])
    a_real = (row_cos * a_scale).astype(jnp.bfloat16)
    a_imag = (-row_sin * a_scale).astype(jnp.bfloat16)
    part_real = product(a_real, t_real) - product(a_imag, t_imag)
    part_imag = product(a_real, t_imag) + product(a_imag, t_real)
    terms = jnp.stack([part_real, part_imag]).reshape(2, band_count, band_count, sub_rows, contrib)
    blocks = lax.psum_scatter(
        terms.astype(jnp.bfloat16), "band", scatter_dimension=2, tiled=True
    ).astype(jnp.float32)
    blocks = lax.psum(blocks, "facet")
    grid_part = blocks.reshape(2, band_count, sub_rows, contrib).astype(jnp.bfloat16)
    tiles = tile_counts.shape[1]
    tile_side = contrib // tiles
    counts = lax.dynamic_slice_in_dim(tile_counts, sub_at * band_count, band_count, 0).astype(
        jnp.float32
    )
    ratio = counts / (counts + 4.0)
    weights = jnp.broadcast_to(
        ratio[:, :, None, :, None], (band_count, tiles, tile_side, tiles, tile_side)
    )
    weights = weights.reshape(band_count, contrib, contrib)
    y_cols = jnp.einsum(
        "ij,cgrj->cgir", kernel, grid_part, preferred_element_type=jnp.float32
    ).astype(jnp.bfloat16)
    y_cols = lax.all_to_all(y_cols, "band", split_axis=2, concat_axis=3, tiled=True)
    z_cols = jnp.einsum("cgqi,ji->cgqj", y_cols, kernel, preferred_element_type=jnp.float32)
    weight_cols = jnp.swapaxes(
        lax.dynamic_slice_in_dim(weights, band_at * sub_rows, sub_rows, 2), 1, 2
    )
    w_cols = (weight_cols[None] * z_cols).astype(jnp.bfloat16)
    u_cols = jnp.einsum("cgqj,jl->cgql", w_cols, kernel, preferred_element_type=jnp.float32).astype(
        jnp.bfloat16
    )
    u_back = lax.all_to_all(u_cols, "band", split_axis=3, concat_axis=2, tiled=True)
    residual_grid = jnp.einsum(
        "cgqr,qm->cgrm", u_back, kernel, preferred_element_type=jnp.float32
    ).astype(jnp.bfloat16)
    back_real = (row_cos * back_scale).astype(jnp.bfloat16).reshape(band_count, contrib, band_rows)
    back_imag = (row_sin * back_scale).astype(jnp.bfloat16).reshape(band_count, contrib, band_rows)
    piece = lax.all_gather(residual_grid, "band", axis=2, tiled=True)
    e_real = jnp.einsum("gkx,gkl->xl", back_real, piece[0], preferred_element_type=jnp.float32)
    e_real = e_real - jnp.einsum(
        "gkx,gkl->xl", back_imag, piece[1], preferred_element_type=jnp.float32
    )
    e_imag = jnp.einsum("gkx,gkl->xl", back_real, piece[1], preferred_element_type=jnp.float32)
    e_imag = e_imag + jnp.einsum(
        "gkx,gkl->xl", back_imag, piece[0], preferred_element_type=jnp.float32
    )
    e_real, e_imag = (e_real, e_imag)
    e_real, e_imag = (
        lax.psum(e_real.astype(jnp.bfloat16), "sub").astype(jnp.float32),
        lax.psum(e_imag.astype(jnp.bfloat16), "sub").astype(jnp.float32),
    )
    out_cos = (cosine * out_scale).astype(jnp.bfloat16)
    out_sin = (sine * out_scale).astype(jnp.bfloat16)
    image = product(e_real.astype(jnp.bfloat16), out_cos) - product(
        e_imag.astype(jnp.bfloat16), out_sin
    )
    return (window[None, :] * image).astype(jnp.bfloat16)


def solution(mesh):
    in_specs = (P(("facet", "band"), None), P(), P(), P(), P(), P(), P())
    out_specs = P(("facet", "band"), None)
    return jax.shard_map(body, mesh=mesh, in_specs=in_specs, out_specs=out_specs, check_vma=False)
```

profile of v0, /device:TPU:0, one launch (start us, length us, event | category | flops | bytes accessed | tf_op | source)
XLA Modules:
  0.0 311.3 jit_solution(18280598410825204298)
XLA Ops:
  7.3 0.8 constant_dynamic-slice_fusion
  8.1 0.5 fusion.138
  8.7 0.7 add_select_fusion.9
  9.3 12.9 %convolution_convert_fusion.3 = bf16[256,512]{1,0:T(8,128)(2,1)} fusion(bf16[512,2048]{1,0:T(8,128)(2,1)S(1)} %copy-done, f32[2048]{0:T(1024)} %param.8, s32[256]{0:T(256)S(1)} %get-tuple-element.14, s32[2048]{0:T(1024)S(1)} %add_select_fusion.9, s32[256]{0:T(256)S(1)} %get-tuple-element.15), kind=kOutput, calls=%fused_computation.73 | convolution fusion | flops 551682048 | bytes 2377728 | tf_op jit(solution)/shard_map/xy,ky->xk/dot_general | solution.py:53
  22.3 10.5 %convolution_convert_fusion.4 = bf16[256,512]{1,0:T(8,128)(2,1)S(1)} fusion(bf16[512,2048]{1,0:T(8,128)(2,1)S(1)} %copy-done, f32[2048]{0:T(1024)S(1)} %copy-done.11, s32[256]{0:T(256)S(1)} %get-tuple-element.14, s32[2048]{0:T(1024)S(1)} %add_select_fusion.9, s32[256]{0:T(256)S(1)} %get-tuple-element.15), kind=kOutput, calls=%fused_computation.74 | convolution fusion | flops 551157760 | bytes 2377728 | tf_op jit(solution)/shard_map/xy,ky->xk/dot_general | solution.py:50
  33.6 10.6 %fusion.58 = f32[1024,256]{1,0:T(8,128)S(1)} fusion(bf16[256,512]{1,0:T(8,128)(2,1)S(1)} %convolution_convert_fusion.4, s32[1024]{0:T(1024)S(1)} %get-tuple-element.8, s32[512]{0:T(512)S(1)} %add_select_fusion.16, s32[1024]{0:T(1024)S(1)} %get-tuple-element.7), kind=kOutput, calls=%fused_computation.88 | convolution fusion | flops 282066944 | bytes 1320960 | tf_op jit(solution)/shard_map/dot_general | solution.py:25
  44.2 10.7 %fusion.57 = f32[1024,256]{1,0:T(8,128)S(1)} fusion(bf16[256,512]{1,0:T(8,128)(2,1)S(1)} %copy-done.14, s32[1024]{0:T(1024)S(1)} %get-tuple-element.8, s32[512]{0:T(512)S(1)} %add_select_fusion.16, s32[1024]{0:T(1024)S(1)} %get-tuple-element.7), kind=kOutput, calls=%fused_computation.87 | convolution fusion | flops 282066944 | bytes 1320960 | tf_op jit(solution)/shard_map/dot_general | solution.py:25
  54.9 11.6 %fusion.36 = bf16[1024,256]{1,0:T(8,128)(2,1)S(1)} fusion(f32[1024,256]{1,0:T(8,128)S(1)} %fusion.58, bf16[256,512]{1,0:T(8,128)(2,1)S(1)} %copy-done.14, s32[1024]{0:T(1024)S(1)} %get-tuple-element.8, s32[512]{0:T(512)S(1)} %add_select_fusion.16, s32[1024]{0:T(1024)S(1)} %get-tuple-element.7), kind=kOutput, calls=%fused_computation.59 | convolution fusion | flops 283115520 | bytes 1845248 | tf_op jit(solution)/shard_map/dot_general | solution.py:25
  66.5 12.0 %fusion.37 = bf16[1024,256]{1,0:T(8,128)(2,1)S(1)} fusion(f32[1024,256]{1,0:T(8,128)S(1)} %fusion.57, bf16[256,512]{1,0:T(8,128)(2,1)S(1)} %convolution_convert_fusion.4, s32[1024]{0:T(1024)S(1)} %get-tuple-element.8, s32[512]{0:T(512)S(1)} %add_select_fusion.16, s32[1024]{0:T(1024)S(1)} %get-tuple-element.7), kind=kOutput, calls=%fused_computation.60 | convolution fusion | flops 283115520 | bytes 1845248 | tf_op jit(solution)/shard_map/dot_general | solution.py:25
  78.6 1.0 copy.25
  79.8 30.1 %reduce-scatter.2.cloned.1.call-done = bf16[2,4,1,64,256]{4,3,1,0,2:T(8,128)(2,1)} async-done(((bf16[2,4,4,64,256]{4,3,1,0,2:T(8,128)(2,1)}), bf16[2,4,1,64,256]{4,3,1,0,2:T(8,128)(2,1)}) %reduce-scatter.2.cloned.1.call-update) | async-done | bytes 262160 | tf_op jit(solution)/shard_map/reduce_scatter | solution.py:65
  109.9 44.5 %all-reduce.4.cloned.1.call-done = bf16[2,4,1,64,256]{4,3,1,0,2:T(8,128)(2,1)} async-done(((bf16[2,4,1,64,256]{4,3,1,0,2:T(8,128)(2,1)}), bf16[2,4,1,64,256]{4,3,1,0,2:T(8,128)(2,1)}) %all-reduce.4.cloned.1.call-update) | async-done | bytes 262160 | tf_op jit(solution)/shard_map/psum | solution.py:68
  154.4 1.2 fusion.43
  155.9 1.1 reshape.290
  157.0 4.6 %all-to-all-start = ((bf16[4,2,16384]{2,1,0:T(2,128)(2,1)}), bf16[4,2,16384]{2,1,0:T(2,128)(2,1)S(1)}, u32[]{:S(2)}, u32[]{:S(2)}) async-start(bf16[4,2,16384]{2,1,0:T(2,128)(2,1)} %reshape.290), calls=%async_computation.1 | async-start | bytes 524288 | tf_op jit(solution)/shard_map/all_to_all | solution.py:83
  161.7 3.9 %broadcast_in_dim.2 = f32[4,16,16,16,16]{2,1,4,3,0:T(8,128)} broadcast(f32[4,16,16]{1,2,0:T(8,128)S(1)} %copy.17), dimensions={0,1,3} | broadcast | bytes 1052672 | tf_op jit(solution)/shard_map/broadcast_in_dim | solution.py:76
  165.6 6.1 %reshape.284 = f32[4,256,256]{1,2,0:T(8,128)S(1)} reshape(f32[4,16,16,16,16]{2,1,4,3,0:T(8,128)} %broadcast_in_dim.2) | data formatting | bytes 2097152 | tf_op jit(solution)/shard_map/reshape | solution.py:79
  171.7 0.7 dynamic-slice_bitcast_fusion
  172.8 0.4 copy.30
  173.6 1.4 convolution_convert_fusion.1
  175.3 0.4 reshape.292
  175.7 12.7 %all_to_all.36 = bf16[4,2,16384]{2,1,0:T(2,128)(2,1)S(1)} all-to-all(bf16[4,2,16384]{2,1,0:T(2,128)(2,1)S(1)} %reshape.292), channel_id=1, replica_groups=mesh['facet'=4,'band'=4,'sub'=2] {'band'}, dimensions={0} | all-to-all | bytes 524288 | tf_op jit(solution)/shard_map/all_to_all | solution.py:92
  188.8 0.4 copy.29
  189.5 0.9 convolution_convert_fusion
  190.7 26.0 %all-gather.2.cloned.1.call-done = bf16[2,4,256,256]{3,2,1,0:T(8,128)(2,1)} async-done(((bf16[2,4,64,256]{3,2,1,0:T(8,128)(2,1)}), bf16[2,4,256,256]{3,2,1,0:T(8,128)(2,1)}) %all-gather.2.cloned.1.call-update) | async-done | bytes 1048592 | tf_op jit(solution)/shard_map/all_gather | solution.py:98
  216.7 11.7 %convolution_bitcast_fusion = f32[512,256]{1,0:T(8,128)S(1)} fusion(s32[4,256]{1,0:T(4,128)S(1)} %get-tuple-element.12, s32[512]{0:T(512)S(1)} %copy-done.4, s32[4,256]{1,0:T(4,128)S(1)} %get-tuple-element.13, bf16[2,4,256,256]{3,2,1,0:T(8,128)(2,1)} %all-gather.2.cloned.1.call-done), kind=kOutput, calls=%fused_computation.61 | convolution fusion | flops 282066944 | bytes 1058816 | tf_op jit(solution)/shard_map/gkx,gkl->xl/dot_general | solution.py:104
  228.4 10.8 %convolution_bitcast_fusion.2 = f32[512,256]{1,0:T(8,128)S(1)} fusion(s32[4,256]{1,0:T(4,128)S(1)} %get-tuple-element.12, s32[512]{0:T(512)S(1)} %copy-done.4, s32[4,256]{1,0:T(4,128)S(1)} %get-tuple-element.13, bf16[2,4,256,256]{3,2,1,0:T(8,128)(2,1)S(1)} %copy-done.9), kind=kOutput, calls=%fused_computation.63 | convolution fusion | flops 282066944 | bytes 1058816 | tf_op jit(solution)/shard_map/gkx,gkl->xl/dot_general | solution.py:100
  239.2 11.6 %fusion.40 = bf16[512,256]{1,0:T(8,128)(2,1)} fusion(f32[512,256]{1,0:T(8,128)S(1)} %convolution_bitcast_fusion, s32[4,256]{1,0:T(4,128)S(1)} %get-tuple-element.12, s32[512]{0:T(512)S(1)} %copy-done.4, s32[4,256]{1,0:T(4,128)S(1)} %get-tuple-element.13, bf16[2,4,256,256]{3,2,1,0:T(8,128)(2,1)S(1)} %copy-done.9), kind=kOutput, calls=%fused_computation.68 | convolution fusion | flops 282329088 | bytes 1320960 | tf_op jit(solution)/shard_map/gkx,gkl->xl/dot_general | solution.py:103
  250.7 11.4 %fusion.41 = bf16[512,256]{1,0:T(8,128)(2,1)} fusion(f32[512,256]{1,0:T(8,128)S(1)} %convolution_bitcast_fusion.2, s32[4,256]{1,0:T(4,128)S(1)} %get-tuple-element.12, s32[512]{0:T(512)S(1)} %copy-done.4, s32[4,256]{1,0:T(4,128)S(1)} %get-tuple-element.13, bf16[2,4,256,256]{3,2,1,0:T(8,128)(2,1)S(1)} %copy-done.9), kind=kOutput, calls=%fused_computation.69 | convolution fusion | flops 282329088 | bytes 1320960 | tf_op jit(solution)/shard_map/gkx,gkl->xl/dot_general | solution.py:99
  262.1 18.2 %all-reduce.6.cloned.1.call-done = (bf16[512,256]{1,0:T(8,128)(2,1)}, bf16[512,256]{1,0:T(8,128)(2,1)}) async-done(((bf16[512,256]{1,0:T(8,128)(2,1)}, bf16[512,256]{1,0:T(8,128)(2,1)}), (bf16[512,256]{1,0:T(8,128)(2,1)}, bf16[512,256]{1,0:T(8,128)(2,1)})) %all-reduce.6.cloned.1.call-update) | async-done | bytes 524304 | tf_op jit(solution)/shard_map/psum | solution.py:109
  280.4 11.8 %fusion.44 = f32[512,2048]{1,0:T(8,128)S(1)} fusion(bf16[512,256]{1,0:T(8,128)(2,1)} %get-tuple-element.5, s32[256]{0:T(256)S(1)} %copy-done.6, s32[2048]{0:T(1024)S(1)} %add_select_fusion.9, s32[256]{0:T(256)S(1)} %copy-done.8), kind=kOutput, calls=%fused_computation.77 | convolution fusion | flops 550502400 | bytes 4466688 | tf_op jit(solution)/shard_map/dot_general | solution.py:25
  292.1 12.3 %multiply_convert_fusion = bf16[512,2048]{1,0:T(8,128)(2,1)} fusion(f32[512,2048]{1,0:T(8,128)S(1)} %fusion.44, bf16[512,256]{1,0:T(8,128)(2,1)S(1)} %copy-done.10, f32[2048]{0:T(1024)S(1)} %copy-done.12, s32[256]{0:T(256)S(1)} %copy-done.6, s32[2048]{0:T(1024)S(1)} %add_select_fusion.9, s32[256]{0:T(256)S(1)} %copy-done.8), kind=kOutput, calls=%fused_computation | convolution fusion | flops 553648128 | bytes 6572032 | tf_op jit(solution)/shard_map/dot_general | solution.py:25
  (54 shorter events, 2.8 us)
Async XLA Ops:
  6.5 2.8 copy-start
  6.5 103.3 %reduce-scatter.2.cloned.1.call-start = ((), (), s32[]{:S(2)}) async-start(), calls=%async_computation.3 | async-start | bytes 1310720 | tf_op jit(solution)/shard_map/reduce_scatter | solution.py:65
  8.6 13.6 %copy-start.5 = (s32[256]{0:T(256)}, s32[256]{0:T(256)S(1)}, u32[]{:S(2)}) copy-start(s32[256]{0:T(256)S(1)} %get-tuple-element.14) | copy-start | bytes 3076
  8.6 13.6 %copy-start.7 = (s32[256]{0:T(256)}, s32[256]{0:T(256)S(1)}, u32[]{:S(2)}) copy-start(s32[256]{0:T(256)S(1)} %get-tuple-element.15) | copy-start | bytes 3076
  9.3 12.9 %copy-start.11 = (f32[2048]{0:T(1024)S(1)}, f32[2048]{0:T(1024)}, u32[]{:S(2)}) copy-start(f32[2048]{0:T(1024)} %param.8) | copy-start | bytes 24580
  22.3 11.1 %copy-start.13 = (s32[8]{0:T(128)S(1)}, s32[8]{0:T(128)}, u32[]{:S(2)}) copy-start(s32[8]{0:T(128)} %param.10) | copy-start | bytes 100
  33.4 33.1 %copy-start.3 = (s32[512]{0:T(512)}, s32[512]{0:T(512)S(1)}, u32[]{:S(2)}) copy-start(s32[512]{0:T(512)S(1)} %add_select_fusion.16) | copy-start | bytes 6148
  33.6 10.6 %copy-start.14 = (bf16[256,512]{1,0:T(8,128)(2,1)S(1)}, bf16[256,512]{1,0:T(8,128)(2,1)}, u32[]{:S(2)}) copy-start(bf16[256,512]{1,0:T(8,128)(2,1)} %convolution_convert_fusion.3) | copy-start | bytes 786436
  78.6 75.8 %copy-start.1 = (bf16[256,256]{1,0:T(8,128)(2,1)S(1)}, bf16[256,256]{1,0:T(8,128)(2,1)}, u32[]{:S(2)}) copy-start(bf16[256,256]{1,0:T(8,128)(2,1)} %param.12) | copy-start | bytes 393220
  79.7 82.0 %copy-start.2 = (s32[8,16,16]{2,1,0:T(8,128)S(1)}, s32[8,16,16]{2,1,0:T(8,128)}, u32[]{:S(2)}) copy-start(s32[8,16,16]{2,1,0:T(8,128)} %param.13) | copy-start | bytes 24580
  79.7 74.7 %all-reduce.4.cloned.1.call-start = ((), (), s32[]{:S(2)}) async-start(), calls=%async_computation.4 | async-start | bytes 524288 | tf_op jit(solution)/shard_map/psum | solution.py:68
  157.0 15.4 %all-to-all-start = ((bf16[4,2,16384]{2,1,0:T(2,128)(2,1)}), bf16[4,2,16384]{2,1,0:T(2,128)(2,1)S(1)}, u32[]{:S(2)}, u32[]{:S(2)}) async-start(bf16[4,2,16384]{2,1,0:T(2,128)(2,1)} %reshape.290), calls=%async_computation.1 | async-start | bytes 524288 | tf_op jit(solution)/shard_map/all_to_all | solution.py:83
  161.6 55.1 %all-gather.2.cloned.1.call-start = ((), (), s32[]{:S(2)}) async-start(), calls=%async_computation.5 | async-start | bytes 1310720 | tf_op jit(solution)/shard_map/all_gather | solution.py:98
  175.7 41.1 %copy-start.4 = (s32[512]{0:T(512)S(1)}, s32[512]{0:T(512)}, u32[]{:S(2)}) copy-start(s32[512]{0:T(512)} %copy-done.3) | copy-start | bytes 6148
  190.5 89.9 %all-reduce.6.cloned.1.call-start = ((), (), s32[]{:S(2)}) async-start(), calls=%async_computation.6 | async-start | bytes 1048576 | tf_op jit(solution)/shard_map/psum | solution.py:109
  216.7 11.7 %copy-start.9 = (bf16[2,4,256,256]{3,2,1,0:T(8,128)(2,1)S(1)}, bf16[2,4,256,256]{3,2,1,0:T(8,128)(2,1)}, u32[]{:S(2)}) copy-start(bf16[2,4,256,256]{3,2,1,0:T(8,128)(2,1)} %all-gather.2.cloned.1.call-done) | copy-start | bytes 3145732
  250.7 29.6 %copy-start.6 = (s32[256]{0:T(256)S(1)}, s32[256]{0:T(256)}, u32[]{:S(2)}) copy-start(s32[256]{0:T(256)} %copy-done.5) | copy-start | bytes 3076
  250.7 29.6 %copy-start.8 = (s32[256]{0:T(256)S(1)}, s32[256]{0:T(256)}, u32[]{:S(2)}) copy-start(s32[256]{0:T(256)} %copy-done.7) | copy-start | bytes 3076
  280.3 11.8 %copy-start.10 = (bf16[512,256]{1,0:T(8,128)(2,1)S(1)}, bf16[512,256]{1,0:T(8,128)(2,1)}, u32[]{:S(2)}) copy-start(bf16[512,256]{1,0:T(8,128)(2,1)} %get-tuple-element.6) | copy-start | bytes 786436
  280.3 11.8 %copy-start.12 = (f32[2048]{0:T(1024)S(1)}, f32[2048]{0:T(1024)}, u32[]{:S(2)}) copy-start(f32[2048]{0:T(1024)} %param.8) | copy-start | bytes 24580
Sparse Core Ops, SparseCore 0:
  79.8 29.9 reduce-scatter.1
  112.8 41.5 all-reduce.3
  190.6 26.0 all-gather.1
  262.3 18.0 all-reduce.5
where the time goes:
time: 316 us; the launch traced here: 311 us
  matrix products  141 us (45%)
  waiting for transfers between devices  119 us (38%)
  local copies, waits for them, and re-layouts  17.5 us (6%)
  between operations  15.1 us (5%)
  blocking collectives  12.7 us (4%)
  starting transfers between devices  4.85 us (2%)
    dot_general x6, matrix products, product(): return jnp.dot(left, right, preferred_element_type=jnp.float32)  69 us
    psum x1, waiting for transfers between devices, body(): blocks = lax.psum(blocks, 'facet')  44.5 us
    reduce_scatter x1, waiting for transfers between devices, body(): lax.psum_scatter(terms.astype(jnp.bfloat16), 'band', scatter_dimension=2,...  30.1 us
    all_gather x1, waiting for transfers between devices, body(): piece = lax.all_gather(residual_grid, 'band', axis=2, tiled=True)  26 us
    psum x1, waiting for transfers between devices, body(): lax.psum(e_real.astype(jnp.bfloat16), 'sub').astype(jnp.float32)  18.2 us
    dot_general x1, matrix products, body(): jnp.einsum('xy,ky->xk', facets, col_imag, preferred_element_type=jnp.floa...  12.9 us
    all_to_all x1, blocking collectives, body(): lax.all_to_all(u_cols, 'band', split_axis=3, concat_axis=2, tiled=True)  12.7 us
    dot_general x1, matrix products, body(): jnp.einsum('gkx,gkl->xl', back_imag, piece[0], preferred_element_type=jnp...  11.7 us
  transfers between devices with their start and end apart: 5, of which 4 were waited for; matrix products, arithmetic and copies ran while one was open for 3% of the time, Pallas kernels for 0%

commit v1 on v0

--- a/solution.py
+++ b/solution.py
@@ -65,7 +65,9 @@
     blocks = lax.psum_scatter(
         terms.astype(jnp.bfloat16), "band", scatter_dimension=2, tiled=True
     ).astype(jnp.float32)
-    blocks = lax.psum(blocks, "facet")
+    blocks = blocks
+    for hop in (1, 2):
+        blocks = blocks + lax.ppermute(blocks, "facet", [(dev, dev ^ hop) for dev in range(4)])
     grid_part = blocks.reshape(2, band_count, sub_rows, contrib).astype(jnp.bfloat16)
     tiles = tile_counts.shape[1]
     tile_side = contrib // tiles

time: 316 us -> 298 us (0.943)
  waiting for transfers between devices: 119 us -> 98.2 us
    psum x1 -> x0, waiting for transfers between devices: 44.5 us -> none  [body(): blocks = lax.psum(blocks, 'facet')]
    ppermute x0 -> x2, waiting for transfers between devices: none -> 22.8 us  [body(): lax.ppermute(blocks, 'facet', [(dev, dev ^ hop) for dev in range(4)])]
  transfers between devices with their start and end apart: 5 -> 6, of which waited for: 4 -> 5; matrix products, arithmetic and copies ran while one was open for 3% -> 4% of each run, Pallas kernels for 0% -> 0%
where the time goes in v1:
time: 298 us; the launch traced here: 293 us
  matrix products  140 us (47%)
  waiting for transfers between devices  98.2 us (33%)
  local copies, waits for them, and re-layouts  17.6 us (6%)
  between operations  15.2 us (5%)
  blocking collectives  11.9 us (4%)
  starting transfers between devices  6.75 us (2%)
    dot_general x6, matrix products, product(): return jnp.dot(left, right, preferred_element_type=jnp.float32)  69 us
    reduce_scatter x1, waiting for transfers between devices, body(): lax.psum_scatter(terms.astype(jnp.bfloat16), 'band', scatter_dimension=2,...  30.2 us
    all_gather x1, waiting for transfers between devices, body(): piece = lax.all_gather(residual_grid, 'band', axis=2, tiled=True)  27.1 us
    ppermute x2, waiting for transfers between devices, body(): lax.ppermute(blocks, 'facet', [(dev, dev ^ hop) for dev in range(4)])  22.8 us
    psum x1, waiting for transfers between devices, body(): lax.psum(e_real.astype(jnp.bfloat16), 'sub').astype(jnp.float32)  18.2 us
    dot_general x1, matrix products, body(): jnp.einsum('xy,ky->xk', facets, col_imag, preferred_element_type=jnp.floa...  12.9 us
    all_to_all x1, blocking collectives, body(): lax.all_to_all(u_cols, 'band', split_axis=3, concat_axis=2, tiled=True)  11.9 us
    dot_general x1, matrix products, body(): jnp.einsum('gkx,gkl->xl', back_imag, piece[0], preferred_element_type=jnp...  11.7 us
  transfers between devices with their start and end apart: 6, of which 5 were waited for; matrix products, arithmetic and copies ran while one was open for 4% of the time, Pallas kernels for 0%

profile of v1, /device:TPU:0, one launch (start us, length us, event | category | flops | bytes accessed | tf_op | source)
XLA Modules:
  0.0 293.0 jit_solution(7507359886808642962)
XLA Ops:
  7.3 0.8 constant_dynamic-slice_fusion
  8.7 0.7 add_select_fusion.9
  9.4 12.9 %convolution_convert_fusion.3 = bf16[256,512]{1,0:T(8,128)(2,1)} fusion(bf16[512,2048]{1,0:T(8,128)(2,1)S(1)} %copy-done, f32[2048]{0:T(1024)} %param.8, s32[256]{0:T(256)S(1)} %get-tuple-element.14, s32[2048]{0:T(1024)S(1)} %add_select_fusion.9, s32[256]{0:T(256)S(1)} %get-tuple-element.15), kind=kOutput, calls=%fused_computation.73 | convolution fusion | flops 551682048 | bytes 2377728 | tf_op jit(solution)/shard_map/xy,ky->xk/dot_general | solution.py:53
  22.3 10.5 %convolution_convert_fusion.4 = bf16[256,512]{1,0:T(8,128)(2,1)S(1)} fusion(bf16[512,2048]{1,0:T(8,128)(2,1)S(1)} %copy-done, f32[2048]{0:T(1024)S(1)} %copy-done.11, s32[256]{0:T(256)S(1)} %get-tuple-element.14, s32[2048]{0:T(1024)S(1)} %add_select_fusion.9, s32[256]{0:T(256)S(1)} %get-tuple-element.15), kind=kOutput, calls=%fused_computation.74 | convolution fusion | flops 551157760 | bytes 2377728 | tf_op jit(solution)/shard_map/xy,ky->xk/dot_general | solution.py:50
  33.8 10.6 %fusion.58 = f32[1024,256]{1,0:T(8,128)S(1)} fusion(bf16[256,512]{1,0:T(8,128)(2,1)S(1)} %convolution_convert_fusion.4, s32[1024]{0:T(1024)S(1)} %get-tuple-element.8, s32[512]{0:T(512)S(1)} %add_select_fusion.16, s32[1024]{0:T(1024)S(1)} %get-tuple-element.7), kind=kOutput, calls=%fused_computation.88 | convolution fusion | flops 282066944 | bytes 1320960 | tf_op jit(solution)/shard_map/dot_general | solution.py:25
  44.4 10.7 %fusion.57 = f32[1024,256]{1,0:T(8,128)S(1)} fusion(bf16[256,512]{1,0:T(8,128)(2,1)S(1)} %copy-done.14, s32[1024]{0:T(1024)S(1)} %get-tuple-element.8, s32[512]{0:T(512)S(1)} %add_select_fusion.16, s32[1024]{0:T(1024)S(1)} %get-tuple-element.7), kind=kOutput, calls=%fused_computation.87 | convolution fusion | flops 282066944 | bytes 1320960 | tf_op jit(solution)/shard_map/dot_general | solution.py:25
  55.1 11.6 %fusion.36 = bf16[1024,256]{1,0:T(8,128)(2,1)S(1)} fusion(f32[1024,256]{1,0:T(8,128)S(1)} %fusion.58, bf16[256,512]{1,0:T(8,128)(2,1)S(1)} %copy-done.14, s32[1024]{0:T(1024)S(1)} %get-tuple-element.8, s32[512]{0:T(512)S(1)} %add_select_fusion.16, s32[1024]{0:T(1024)S(1)} %get-tuple-element.7), kind=kOutput, calls=%fused_computation.59 | convolution fusion | flops 283115520 | bytes 1845248 | tf_op jit(solution)/shard_map/dot_general | solution.py:25
  66.7 12.0 %fusion.37 = bf16[1024,256]{1,0:T(8,128)(2,1)S(1)} fusion(f32[1024,256]{1,0:T(8,128)S(1)} %fusion.57, bf16[256,512]{1,0:T(8,128)(2,1)S(1)} %convolution_convert_fusion.4, s32[1024]{0:T(1024)S(1)} %get-tuple-element.8, s32[512]{0:T(512)S(1)} %add_select_fusion.16, s32[1024]{0:T(1024)S(1)} %get-tuple-element.7), kind=kOutput, calls=%fused_computation.60 | convolution fusion | flops 283115520 | bytes 1845248 | tf_op jit(solution)/shard_map/dot_general | solution.py:25
  78.8 1.0 copy.25
  79.9 30.2 %reduce-scatter.2.cloned.1.call-done = bf16[2,4,1,64,256]{4,3,1,0,2:T(8,128)(2,1)} async-done(((bf16[2,4,4,64,256]{4,3,1,0,2:T(8,128)(2,1)}), bf16[2,4,1,64,256]{4,3,1,0,2:T(8,128)(2,1)}) %reduce-scatter.2.cloned.1.call-update) | async-done | bytes 262160 | tf_op jit(solution)/shard_map/reduce_scatter | solution.py:65
  110.0 1.0 convert_element_type.115
  111.0 1.5 collective-permute-start
  112.6 11.8 %collective-permute-done = f32[2,4,1,64,256]{4,3,1,0,2:T(8,128)S(1)} collective-permute-done((f32[2,4,1,64,256]{4,3,1,0,2:T(8,128)S(1)}, f32[2,4,1,64,256]{4,3,1,0,2:T(8,128)S(1)}, u32[]{:S(2)}, u32[]{:S(2)}) %collective-permute-start) | collective-permute-done | bytes 524320 | tf_op jit(solution)/shard_map/ppermute | solution.py:70
  124.4 1.0 convert_add_fusion
  125.4 1.5 collective-permute-start.1
  126.9 11.0 %collective-permute-done.1 = f32[2,4,1,64,256]{4,3,1,0,2:T(8,128)S(1)} collective-permute-done((f32[2,4,1,64,256]{4,3,1,0,2:T(8,128)S(1)}, f32[2,4,1,64,256]{4,3,1,0,2:T(8,128)S(1)}, u32[]{:S(2)}, u32[]{:S(2)}) %collective-permute-start.1) | collective-permute-done | bytes 524320 | tf_op jit(solution)/shard_map/ppermute | solution.py:70
  138.5 1.1 reshape.290
  139.6 3.4 %all-to-all-start = ((bf16[4,2,16384]{2,1,0:T(2,128)(2,1)}), bf16[4,2,16384]{2,1,0:T(2,128)(2,1)S(1)}, u32[]{:S(2)}, u32[]{:S(2)}) async-start(bf16[4,2,16384]{2,1,0:T(2,128)(2,1)} %reshape.290), calls=%async_computation.1 | async-start | bytes 524288 | tf_op jit(solution)/shard_map/all_to_all | solution.py:85
  143.2 3.9 %broadcast_in_dim.2 = f32[4,16,16,16,16]{2,1,4,3,0:T(8,128)} broadcast(f32[4,16,16]{1,2,0:T(8,128)S(1)} %copy.17), dimensions={0,1,3} | broadcast | bytes 1052672 | tf_op jit(solution)/shard_map/broadcast_in_dim | solution.py:78
  147.1 6.1 %reshape.284 = f32[4,256,256]{1,2,0:T(8,128)S(1)} reshape(f32[4,16,16,16,16]{2,1,4,3,0:T(8,128)} %broadcast_in_dim.2) | data formatting | bytes 2097152 | tf_op jit(solution)/shard_map/reshape | solution.py:81
  153.2 0.7 dynamic-slice_bitcast_fusion
  155.0 1.4 convolution_convert_fusion.1
  157.2 11.9 %all_to_all.36 = bf16[4,2,16384]{2,1,0:T(2,128)(2,1)S(1)} all-to-all(bf16[4,2,16384]{2,1,0:T(2,128)(2,1)S(1)} %reshape.292), channel_id=1, replica_groups=mesh['facet'=4,'band'=4,'sub'=2] {'band'}, dimensions={0} | all-to-all | bytes 524288 | tf_op jit(solution)/shard_map/all_to_all | solution.py:94
  170.2 0.9 convolution_convert_fusion
  171.4 27.1 %all-gather.2.cloned.1.call-done = bf16[2,4,256,256]{3,2,1,0:T(8,128)(2,1)} async-done(((bf16[2,4,64,256]{3,2,1,0:T(8,128)(2,1)}), bf16[2,4,256,256]{3,2,1,0:T(8,128)(2,1)}) %all-gather.2.cloned.1.call-update) | async-done | bytes 1048592 | tf_op jit(solution)/shard_map/all_gather | solution.py:100
  198.4 11.7 %convolution_bitcast_fusion = f32[512,256]{1,0:T(8,128)S(1)} fusion(s32[4,256]{1,0:T(4,128)S(1)} %get-tuple-element.12, s32[512]{0:T(512)S(1)} %copy-done.4, s32[4,256]{1,0:T(4,128)S(1)} %get-tuple-element.13, bf16[2,4,256,256]{3,2,1,0:T(8,128)(2,1)} %all-gather.2.cloned.1.call-done), kind=kOutput, calls=%fused_computation.61 | convolution fusion | flops 282066944 | bytes 1058816 | tf_op jit(solution)/shard_map/gkx,gkl->xl/dot_general | solution.py:106
  210.1 10.7 %convolution_bitcast_fusion.2 = f32[512,256]{1,0:T(8,128)S(1)} fusion(s32[4,256]{1,0:T(4,128)S(1)} %get-tuple-element.12, s32[512]{0:T(512)S(1)} %copy-done.4, s32[4,256]{1,0:T(4,128)S(1)} %get-tuple-element.13, bf16[2,4,256,256]{3,2,1,0:T(8,128)(2,1)S(1)} %copy-done.9), kind=kOutput, calls=%fused_computation.63 | convolution fusion | flops 282066944 | bytes 1058816 | tf_op jit(solution)/shard_map/gkx,gkl->xl/dot_general | solution.py:102
  220.9 11.6 %fusion.40 = bf16[512,256]{1,0:T(8,128)(2,1)} fusion(f32[512,256]{1,0:T(8,128)S(1)} %convolution_bitcast_fusion, s32[4,256]{1,0:T(4,128)S(1)} %get-tuple-element.12, s32[512]{0:T(512)S(1)} %copy-done.4, s32[4,256]{1,0:T(4,128)S(1)} %get-tuple-element.13, bf16[2,4,256,256]{3,2,1,0:T(8,128)(2,1)S(1)} %copy-done.9), kind=kOutput, calls=%fused_computation.68 | convolution fusion | flops 282329088 | bytes 1320960 | tf_op jit(solution)/shard_map/gkx,gkl->xl/dot_general | solution.py:105
  232.5 11.4 %fusion.41 = bf16[512,256]{1,0:T(8,128)(2,1)} fusion(f32[512,256]{1,0:T(8,128)S(1)} %convolution_bitcast_fusion.2, s32[4,256]{1,0:T(4,128)S(1)} %get-tuple-element.12, s32[512]{0:T(512)S(1)} %copy-done.4, s32[4,256]{1,0:T(4,128)S(1)} %get-tuple-element.13, bf16[2,4,256,256]{3,2,1,0:T(8,128)(2,1)S(1)} %copy-done.9), kind=kOutput, calls=%fused_computation.69 | convolution fusion | flops 282329088 | bytes 1320960 | tf_op jit(solution)/shard_map/gkx,gkl->xl/dot_general | solution.py:101
  243.9 18.2 %all-reduce.3.cloned.1.call-done = (bf16[512,256]{1,0:T(8,128)(2,1)}, bf16[512,256]{1,0:T(8,128)(2,1)}) async-done(((bf16[512,256]{1,0:T(8,128)(2,1)}, bf16[512,256]{1,0:T(8,128)(2,1)}), (bf16[512,256]{1,0:T(8,128)(2,1)}, bf16[512,256]{1,0:T(8,128)(2,1)})) %all-reduce.3.cloned.1.call-update) | async-done | bytes 524304 | tf_op jit(solution)/shard_map/psum | solution.py:111
  262.1 11.8 %fusion.44 = f32[512,2048]{1,0:T(8,128)S(1)} fusion(bf16[512,256]{1,0:T(8,128)(2,1)} %get-tuple-element.5, s32[256]{0:T(256)S(1)} %copy-done.6, s32[2048]{0:T(1024)S(1)} %add_select_fusion.9, s32[256]{0:T(256)S(1)} %copy-done.8), kind=kOutput, calls=%fused_computation.77 | convolution fusion | flops 550502400 | bytes 4466688 | tf_op jit(solution)/shard_map/dot_general | solution.py:25
  273.8 12.3 %multiply_convert_fusion = bf16[512,2048]{1,0:T(8,128)(2,1)} fusion(f32[512,2048]{1,0:T(8,128)S(1)} %fusion.44, bf16[512,256]{1,0:T(8,128)(2,1)S(1)} %copy-done.10, f32[2048]{0:T(1024)S(1)} %copy-done.12, s32[256]{0:T(256)S(1)} %copy-done.6, s32[2048]{0:T(1024)S(1)} %add_select_fusion.9, s32[256]{0:T(256)S(1)} %copy-done.8), kind=kOutput, calls=%fused_computation | convolution fusion | flops 553648128 | bytes 6572032 | tf_op jit(solution)/shard_map/dot_general | solution.py:25
  (57 shorter events, 4.9 us)
Async XLA Ops:
  6.5 2.9 copy-start
  6.5 103.5 %reduce-scatter.2.cloned.1.call-start = ((), (), s32[]{:S(2)}) async-start(), calls=%async_computation.3 | async-start | bytes 1310720 | tf_op jit(solution)/shard_map/reduce_scatter | solution.py:65
  8.7 13.6 %copy-start.5 = (s32[256]{0:T(256)}, s32[256]{0:T(256)S(1)}, u32[]{:S(2)}) copy-start(s32[256]{0:T(256)S(1)} %get-tuple-element.14) | copy-start | bytes 3076
  8.7 13.6 %copy-start.7 = (s32[256]{0:T(256)}, s32[256]{0:T(256)S(1)}, u32[]{:S(2)}) copy-start(s32[256]{0:T(256)S(1)} %get-tuple-element.15) | copy-start | bytes 3076
  9.4 12.9 %copy-start.11 = (f32[2048]{0:T(1024)S(1)}, f32[2048]{0:T(1024)}, u32[]{:S(2)}) copy-start(f32[2048]{0:T(1024)} %param.8) | copy-start | bytes 24580
  22.3 11.2 %copy-start.13 = (s32[8]{0:T(128)S(1)}, s32[8]{0:T(128)}, u32[]{:S(2)}) copy-start(s32[8]{0:T(128)} %param.10) | copy-start | bytes 100
  33.5 33.1 %copy-start.3 = (s32[512]{0:T(512)}, s32[512]{0:T(512)S(1)}, u32[]{:S(2)}) copy-start(s32[512]{0:T(512)S(1)} %add_select_fusion.16) | copy-start | bytes 6148
  33.8 10.6 %copy-start.14 = (bf16[256,512]{1,0:T(8,128)(2,1)S(1)}, bf16[256,512]{1,0:T(8,128)(2,1)}, u32[]{:S(2)}) copy-start(bf16[256,512]{1,0:T(8,128)(2,1)} %convolution_convert_fusion.3) | copy-start | bytes 786436
  79.9 58.1 %copy-start.1 = (bf16[256,256]{1,0:T(8,128)(2,1)S(1)}, bf16[256,256]{1,0:T(8,128)(2,1)}, u32[]{:S(2)}) copy-start(bf16[256,256]{1,0:T(8,128)(2,1)} %param.12) | copy-start | bytes 393220
  111.0 13.4 %collective-permute-start = (f32[2,4,1,64,256]{4,3,1,0,2:T(8,128)S(1)}, f32[2,4,1,64,256]{4,3,1,0,2:T(8,128)S(1)}, u32[]{:S(2)}, u32[]{:S(2)}) collective-permute-start(f32[2,4,1,64,256]{4,3,1,0,2:T(8,128)S(1)} %convert_element_type.115), channel_id=1, source_target_pairs={{0,8},{8,0},{16,24},{24,16},{1,9},{9,1},{17,25},{25,17},{2,10},{10... | collective-permute-start | bytes 1572872 | tf_op jit(solution)/shard_map/ppermute | solution.py:70
  125.4 17.7 %copy-start.2 = (s32[8,16,16]{2,1,0:T(8,128)S(1)}, s32[8,16,16]{2,1,0:T(8,128)}, u32[]{:S(2)}) copy-start(s32[8,16,16]{2,1,0:T(8,128)} %param.13) | copy-start | bytes 24580
  125.4 12.5 %collective-permute-start.1 = (f32[2,4,1,64,256]{4,3,1,0,2:T(8,128)S(1)}, f32[2,4,1,64,256]{4,3,1,0,2:T(8,128)S(1)}, u32[]{:S(2)}, u32[]{:S(2)}) collective-permute-start(f32[2,4,1,64,256]{4,3,1,0,2:T(8,128)S(1)} %convert_add_fusion), channel_id=1, source_target_pairs={{0,16},{8,24},{16,0},{24,8},{1,17},{9,25},{17,1},{25,9},{2,18},{10... | collective-permute-start | bytes 1572872 | tf_op jit(solution)/shard_map/ppermute | solution.py:70
  139.6 14.3 %all-to-all-start = ((bf16[4,2,16384]{2,1,0:T(2,128)(2,1)}), bf16[4,2,16384]{2,1,0:T(2,128)(2,1)S(1)}, u32[]{:S(2)}, u32[]{:S(2)}) async-start(bf16[4,2,16384]{2,1,0:T(2,128)(2,1)} %reshape.290), calls=%async_computation.1 | async-start | bytes 524288 | tf_op jit(solution)/shard_map/all_to_all | solution.py:85
  143.0 55.4 %all-gather.2.cloned.1.call-start = ((), (), s32[]{:S(2)}) async-start(), calls=%async_computation.4 | async-start | bytes 1310720 | tf_op jit(solution)/shard_map/all_gather | solution.py:100
  157.1 41.3 %copy-start.4 = (s32[512]{0:T(512)S(1)}, s32[512]{0:T(512)}, u32[]{:S(2)}) copy-start(s32[512]{0:T(512)} %copy-done.3) | copy-start | bytes 6148
  171.1 90.9 %all-reduce.3.cloned.1.call-start = ((), (), s32[]{:S(2)}) async-start(), calls=%async_computation.5 | async-start | bytes 1048576 | tf_op jit(solution)/shard_map/psum | solution.py:111
  198.4 11.7 %copy-start.9 = (bf16[2,4,256,256]{3,2,1,0:T(8,128)(2,1)S(1)}, bf16[2,4,256,256]{3,2,1,0:T(8,128)(2,1)}, u32[]{:S(2)}) copy-start(bf16[2,4,256,256]{3,2,1,0:T(8,128)(2,1)} %all-gather.2.cloned.1.call-done) | copy-start | bytes 3145732
  232.5 29.6 %copy-start.6 = (s32[256]{0:T(256)S(1)}, s32[256]{0:T(256)}, u32[]{:S(2)}) copy-start(s32[256]{0:T(256)} %copy-done.5) | copy-start | bytes 3076
  232.5 29.6 %copy-start.8 = (s32[256]{0:T(256)S(1)}, s32[256]{0:T(256)}, u32[]{:S(2)}) copy-start(s32[256]{0:T(256)} %copy-done.7) | copy-start | bytes 3076
  262.1 11.8 %copy-start.10 = (bf16[512,256]{1,0:T(8,128)(2,1)S(1)}, bf16[512,256]{1,0:T(8,128)(2,1)}, u32[]{:S(2)}) copy-start(bf16[512,256]{1,0:T(8,128)(2,1)} %get-tuple-element.6) | copy-start | bytes 786436
  262.1 11.8 %copy-start.12 = (f32[2048]{0:T(1024)S(1)}, f32[2048]{0:T(1024)}, u32[]{:S(2)}) copy-start(f32[2048]{0:T(1024)} %param.8) | copy-start | bytes 24580
Sparse Core Ops, SparseCore 0:
  80.0 29.9 reduce-scatter.1
  171.3 27.1 all-gather.1
  244.0 18.0 all-reduce.2
